TPU v7x, 512 devices: a whole 4x4x16 slice. The times are simulated.
512 devices in a mesh: expert: 128 (over y, x, z_lo), hidden: 4 (over z_hi, core).
Axes of the slice: x: 4, y: 4, z: 16 (z_hi: 2, z_lo: 8; z = z_hi * 8 + z_lo), core: 2. Of those that a mesh axis runs over, the one named last changes fastest.
Arguments:
- tokens: bfloat16 [256, 196, 1024], P('expert', None, 'hidden'), may hold values from -64 to 64
- slot_params: bfloat16 [1024, 128], P('hidden'), may hold values from -0.4 to 0.4
- weight_in: bfloat16 [128, 1024, 4096], P('expert', None, 'hidden'), may hold values from -0.1875 to 0.1875
- bias_in: bfloat16 [128, 4096], P('expert', 'hidden'), may hold values from -3 to 3
- weight_out: bfloat16 [128, 4096, 1024], P('expert', 'hidden'), may hold values from -0.09375 to 0.09375
- bias_out: bfloat16 [128, 1024], P('expert', 'hidden'), may hold values from -3 to 3
- cotangent: bfloat16 [256, 196, 1024], P('expert', None, 'hidden'), may hold values from -1.5 to 1.5
Outputs:
- mixed: bfloat16 [256, 196, 1024], P('expert', None, 'hidden')
- token_grad: bfloat16 [256, 196, 1024], P('expert', None, 'hidden')
- zloss: float32 [256, 196], P('expert')
All inputs are finite; a program needn't handle non-finite values.
Results may differ from a plain program's by a relative error of at most 0.015.
Values may be sent and summed in bfloat16 or wider, within the bound.
A program may use at most 64 MiB of HBM per device.

v0:
```python
import jax
import jax.numpy as jnp
from jax import lax
from jax.sharding import PartitionSpec as P

loss_weight = 0.1


def sent_to_all(x, axis):
    copies = jnp.broadcast_to(x, (lax.axis_size(axis), *x.shape))
    return lax.all_to_all(copies, axis, split_axis=0, concat_axis=0, tiled=True)


def of_everyone(x, axis):
    everything = sent_to_all(x, axis)
    return jnp.sum(everything, axis=0)


def in_order(tiles, dim):
    tiles = jnp.moveaxis(tiles, 0, dim)
    lengths = tiles.shape
    return tiles.reshape(*lengths[:dim], lengths[dim] * lengths[dim + 1], *lengths[dim + 2 :])


def gathered_copies(x, axis, dim):
    return in_order(sent_to_all(x, axis), dim)


def split_up(x, dim, peers):
    lengths = x.shape
    tiles = x.reshape(*lengths[:dim], peers, lengths[dim] // peers, *lengths[dim + 1 :])
    return jnp.moveaxis(tiles, dim, 0)


def sent_and_summed(x, axis, dim):
    peers = lax.axis_size(axis)
    tiles = lax.all_to_all(split_up(x, dim, peers), axis, 0, 0, tiled=True)
    return jnp.sum(tiles.astype(jnp.float32), axis=0)


def taken_together(x, axis):
    everything = sent_to_all(x, axis)
    return jnp.sum(everything.astype(jnp.float32), axis=0)


def gelu_parts(value):
    factor = 0.7978845608028654
    inner = factor * (value + 0.044715 * value * value * value)
    slope_tanh = jnp.tanh(inner)
    result = 0.5 * value * (1.0 + slope_tanh)
    slope = 0.5 * (1.0 + slope_tanh) + 0.5 * value * (1.0 - slope_tanh * slope_tanh) * factor * (
        1.0 + 3.0 * 0.044715 * value * value
    )
    return (result, slope)


def per_device(tokens, slot_params, weight_in, bias_in, weight_out, bias_out, cotangent):
    images_dev = tokens.shape[0]
    groups = lax.axis_size("expert")
    local_experts = weight_in.shape[0]
    quarter = tokens.shape[2]
    partial_value = jnp.einsum(
        "itd,ds->its", tokens, slot_params, preferred_element_type=jnp.float32
    )
    logits = of_everyone(partial_value, "hidden")
    dispatch = jax.nn.softmax(logits, axis=1)
    combine = jax.nn.softmax(logits, axis=2)
    log_total = jax.nn.logsumexp(logits, axis=2)
    zloss = loss_weight * log_total * log_total
    dispatch_low = dispatch.astype(jnp.bfloat16)
    combine_low = combine.astype(jnp.bfloat16)
    slot_in = jnp.einsum(
        "its,itd->isd", dispatch_low, tokens, preferred_element_type=jnp.float32
    ).astype(jnp.bfloat16)
    arrived = lax.all_to_all(slot_in, "expert", split_axis=1, concat_axis=0, tiled=True)
    pre_act = jnp.einsum(
        "ren,enf->ref",
        gathered_copies(arrived, "hidden", 2),
        weight_in,
        preferred_element_type=jnp.float32,
    )
    pre_act = pre_act + bias_in.astype(jnp.float32)[None]
    activated, slope = gelu_parts(pre_act)
    act_low = activated.astype(jnp.bfloat16)
    out_terms = jnp.einsum("ref,efd->red", act_low, weight_out, preferred_element_type=jnp.float32)
    expert_out = sent_and_summed(out_terms.astype(jnp.bfloat16), "hidden", 2)
    expert_low = (expert_out + bias_out.astype(jnp.float32)[None]).astype(jnp.bfloat16)
    slot_out = lax.all_to_all(
        expert_low.reshape(groups, images_dev, local_experts, quarter),
        "expert",
        split_axis=0,
        concat_axis=2,
        tiled=True,
    )
    slot_out = slot_out.reshape(images_dev, groups * local_experts, quarter)
    mixed = jnp.einsum(
        "its,isd->itd", combine_low, slot_out, preferred_element_type=jnp.float32
    ).astype(jnp.bfloat16)
    combine_part = jnp.einsum(
        "itd,isd->its", cotangent, slot_out, preferred_element_type=jnp.float32
    )
    out_grad = jnp.einsum(
        "its,itd->isd", combine_low, cotangent, preferred_element_type=jnp.float32
    ).astype(jnp.bfloat16)
    grad_arrived = lax.all_to_all(out_grad, "expert", split_axis=1, concat_axis=0, tiled=True)
    hidden_grad = jnp.einsum(
        "ren,efn->ref",
        gathered_copies(grad_arrived, "hidden", 2),
        weight_out,
        preferred_element_type=jnp.float32,
    )
    pre_grad = (hidden_grad * slope).astype(jnp.bfloat16)
    in_terms = jnp.einsum("ref,ekf->rek", pre_grad, weight_in, preferred_element_type=jnp.float32)
    slot_grad = sent_and_summed(in_terms.astype(jnp.bfloat16), "hidden", 2).astype(jnp.bfloat16)
    in_grad = lax.all_to_all(
        slot_grad.reshape(groups, images_dev, local_experts, quarter),
        "expert",
        split_axis=0,
        concat_axis=2,
        tiled=True,
    )
    in_grad = in_grad.reshape(images_dev, groups * local_experts, quarter)
    dispatch_part = jnp.einsum("itd,isd->its", tokens, in_grad, preferred_element_type=jnp.float32)
    combine_grad, dispatch_grad = (
        taken_together(combine_part.astype(jnp.bfloat16), "hidden").astype(jnp.float32),
        taken_together(dispatch_part.astype(jnp.bfloat16), "hidden").astype(jnp.float32),
    )
    from_combine = (
        combine * (combine_grad - jnp.sum(combine * combine_grad, axis=2, keepdims=True))
        + 2.0 * loss_weight * log_total[:, :, None] * combine
    )
    from_dispatch = dispatch * (
        dispatch_grad - jnp.sum(dispatch * dispatch_grad, axis=1, keepdims=True)
    )
    logit_low = (from_combine + from_dispatch).astype(jnp.bfloat16)
    token_grad = jnp.einsum(
        "its,ds->itd", logit_low, slot_params, preferred_element_type=jnp.float32
    )
    token_grad = token_grad + jnp.einsum(
        "its,isd->itd", dispatch_low, in_grad, preferred_element_type=jnp.float32
    )
    return (mixed, token_grad.astype(jnp.bfloat16), zloss)


def solution(mesh):
    return jax.shard_map(
        per_device,
        mesh=mesh,
        in_specs=(
            P("expert", None, "hidden"),
            P("hidden", None),
            P("expert", None, "hidden"),
            P("expert", "hidden"),
            P("expert", "hidden", None),
            P("expert", "hidden"),
            P("expert", None, "hidden"),
        ),
        out_specs=(P("expert", None, "hidden"), P("expert", None, "hidden"), P("expert", None)),
        check_vma=False,
    )
```

profile of v0, /device:TPU:49, one launch (start us, length us, event | category | flops | bytes accessed | tf_op | source)
XLA Modules:
  0.0 364.0 jit_solution(17710383384347243278)
XLA Ops:
  0.6 1.3 fusion.66
  2.3 60.5 %all_to_all.101 = f32[4,2,196,128]{3,1,2,0:T(2,128)S(1)} all-to-all(f32[4,2,196,128]{3,1,2,0:T(2,128)S(1)} %broadcast_in_dim.12), channel_id=1, replica_groups=mesh['expert'=128,'hidden'=4] {'hidden'}, dimensions={0} | all-to-all | bytes 1605632 | tf_op jit(solution)/shard_map/all_to_all | solution.py:11
  63.5 0.9 exponential_reduce_fusion
  64.4 1.2 fusion.99
  65.6 1.2 convolution_convert_fusion.2
  66.8 0.8 copy.114
  67.6 11.5 %all-to-all-start.1 = ((bf16[2,128,256]{2,0,1:T(2,128)(2,1)}), bf16[2,128,256]{2,0,1:T(2,128)(2,1)S(1)}, u32[]{:S(2)}, u32[]{:S(2)}) async-start(bf16[2,128,256]{2,0,1:T(2,128)(2,1)} %copy.114), calls=%async_computation.1 | async-start | bytes 262144 | tf_op jit(solution)/shard_map/all_to_all | solution.py:75
  79.4 0.8 copy.126
  80.1 10.7 %all-to-all-done.1 = bf16[2,128,256]{2,0,1:T(2,128)(2,1)S(1)} async-done(((bf16[2,128,256]{2,0,1:T(2,128)(2,1)}), bf16[2,128,256]{2,0,1:T(2,128)(2,1)S(1)}, u32[]{:S(2)}, u32[]{:S(2)}) %all-to-all-start.1) | async-done | bytes 131104 | tf_op jit(solution)/shard_map/all_to_all | solution.py:75
  90.8 11.6 %all-to-all-start.6 = ((bf16[2,128,256]{2,0,1:T(2,128)(2,1)}), bf16[2,128,256]{2,0,1:T(2,128)(2,1)S(1)}, u32[]{:S(2)}, u32[]{:S(2)}) async-start(bf16[2,128,256]{2,0,1:T(2,128)(2,1)} %copy.126), calls=%async_computation.6 | async-start | bytes 262144 | tf_op jit(solution)/shard_map/all_to_all | solution.py:105
  102.5 11.5 %all-to-all-done.6 = bf16[2,128,256]{2,0,1:T(2,128)(2,1)S(1)} async-done(((bf16[2,128,256]{2,0,1:T(2,128)(2,1)}), bf16[2,128,256]{2,0,1:T(2,128)(2,1)S(1)}, u32[]{:S(2)}, u32[]{:S(2)}) %all-to-all-start.6) | async-done | bytes 131104 | tf_op jit(solution)/shard_map/all_to_all | solution.py:105
  114.1 0.8 broadcast_in_dim.13
  114.9 6.3 %all-to-all-start.2 = ((bf16[4,256,1,256]{1,3,2,0:T(8,128)(2,1)}), bf16[4,256,1,256]{1,3,2,0:T(8,128)(2,1)S(1)}, u32[]{:S(2)}, u32[]{:S(2)}) async-start(bf16[4,256,1,256]{1,3,2,0:T(8,128)(2,1)} %broadcast_in_dim.13), calls=%async_computation.2 | async-start | bytes 1048576 | tf_op jit(solution)/shard_map/all_to_all | solution.py:11
  121.4 33.5 %all-to-all-done.2 = bf16[4,256,1,256]{1,3,2,0:T(8,128)(2,1)S(1)} async-done(((bf16[4,256,1,256]{1,3,2,0:T(8,128)(2,1)}), bf16[4,256,1,256]{1,3,2,0:T(8,128)(2,1)S(1)}, u32[]{:S(2)}, u32[]{:S(2)}) %all-to-all-start.2) | async-done | bytes 524320 | tf_op jit(solution)/shard_map/all_to_all | solution.py:11
  154.8 0.9 broadcast_in_dim.32
  155.7 4.0 %all-to-all-start.7 = ((bf16[4,256,1,256]{1,3,2,0:T(8,128)(2,1)}), bf16[4,256,1,256]{1,3,2,0:T(8,128)(2,1)S(1)}, u32[]{:S(2)}, u32[]{:S(2)}) async-start(bf16[4,256,1,256]{1,3,2,0:T(8,128)(2,1)} %broadcast_in_dim.32), calls=%async_computation.7 | async-start | bytes 1048576 | tf_op jit(solution)/shard_map/all_to_all | solution.py:11
  159.7 0.7 add.77
  160.4 1.7 fusion.21
  162.1 19.1 %all-to-all-done.7 = bf16[4,256,1,256]{1,3,2,0:T(8,128)(2,1)S(1)} async-done(((bf16[4,256,1,256]{1,3,2,0:T(8,128)(2,1)}), bf16[4,256,1,256]{1,3,2,0:T(8,128)(2,1)S(1)}, u32[]{:S(2)}, u32[]{:S(2)}) %all-to-all-start.7) | async-done | bytes 524320 | tf_op jit(solution)/shard_map/all_to_all | solution.py:11
  181.2 3.7 %fusion.24 = bf16[256,1024]{1,0:T(8,128)(2,1)S(1)} fusion(bf16[1,1024,1024]{2,1,0:T(8,128)(2,1)S(1)} %copy-done, bf16[256,1024]{0,1:T(8,128)(2,1)S(1)} %bitcast.139, bf16[1,1024,1024]{2,1,0:T(8,128)(2,1)} %param.11, f32[256,1,1024]{2,0,1:T(8,128)} %fusion.21), kind=kOutput, calls=%fused_computation.16 | convolution fusion | flops 1078984704 | bytes 6291456 | tf_op jit(solution)/shard_map/ref,ekf->rek/dot_general | solution.py:113
  184.9 0.9 copy.182
  185.8 8.2 %all-to-all-start.8 = ((bf16[4,256,1,256]{3,1,2,0:T(8,128)(2,1)}), bf16[4,256,1,256]{3,1,2,0:T(8,128)(2,1)S(1)}, u32[]{:S(2)}, u32[]{:S(2)}) async-start(bf16[4,256,1,256]{3,1,2,0:T(8,128)(2,1)} %bitcast.134), calls=%async_computation.8 | async-start | bytes 1048576 | tf_op jit(solution)/shard_map/all_to_all | solution.py:37
  194.0 2.7 fusion.27
  196.7 0.8 copy.183
  197.6 18.0 %all-to-all-done.8 = bf16[4,256,1,256]{3,1,2,0:T(8,128)(2,1)S(1)} async-done(((bf16[4,256,1,256]{3,1,2,0:T(8,128)(2,1)}), bf16[4,256,1,256]{3,1,2,0:T(8,128)(2,1)S(1)}, u32[]{:S(2)}, u32[]{:S(2)}) %all-to-all-start.8) | async-done | bytes 524320 | tf_op jit(solution)/shard_map/all_to_all | solution.py:37
  215.6 4.1 %all-to-all-start.3 = ((bf16[4,256,1,256]{3,1,2,0:T(8,128)(2,1)}), bf16[4,256,1,256]{3,1,2,0:T(8,128)(2,1)S(1)}, u32[]{:S(2)}, u32[]{:S(2)}) async-start(bf16[4,256,1,256]{3,1,2,0:T(8,128)(2,1)} %bitcast.138), calls=%async_computation.3 | async-start | bytes 1048576 | tf_op jit(solution)/shard_map/all_to_all | solution.py:37
  219.7 0.7 reduce_sum.103
  220.4 1.6 reshape.121
  222.0 18.7 %all-to-all-done.3 = bf16[4,256,1,256]{3,1,2,0:T(8,128)(2,1)S(1)} async-done(((bf16[4,256,1,256]{3,1,2,0:T(8,128)(2,1)}), bf16[4,256,1,256]{3,1,2,0:T(8,128)(2,1)S(1)}, u32[]{:S(2)}, u32[]{:S(2)}) %all-to-all-start.3) | async-done | bytes 524320 | tf_op jit(solution)/shard_map/all_to_all | solution.py:37
  240.8 18.6 %all-to-all-start.9 = ((bf16[128,2,1,256]{3,1,2,0:T(2,128)(2,1)}), bf16[128,2,1,256]{3,1,2,0:T(2,128)(2,1)}, u32[]{:S(2)}, u32[]{:S(2)}) async-start(bf16[128,2,1,256]{3,1,2,0:T(2,128)(2,1)} %bitcast.37), calls=%async_computation.9 | async-start | bytes 262144 | tf_op jit(solution)/shard_map/all_to_all | solution.py:115
  259.4 1.2 convert_element_type.119
  260.9 0.7 fusion.61
  261.6 0.8 copy.119
  262.4 9.7 %all-to-all-done.9 = bf16[128,2,1,256]{3,1,2,0:T(2,128)(2,1)} async-done(((bf16[128,2,1,256]{3,1,2,0:T(2,128)(2,1)}), bf16[128,2,1,256]{3,1,2,0:T(2,128)(2,1)}, u32[]{:S(2)}, u32[]{:S(2)}) %all-to-all-start.9) | async-done | bytes 131104 | tf_op jit(solution)/shard_map/all_to_all | solution.py:115
  272.1 10.3 %all-to-all-start.4 = ((bf16[128,2,1,256]{3,1,2,0:T(2,128)(2,1)}), bf16[128,2,1,256]{3,1,2,0:T(2,128)(2,1)S(1)}, u32[]{:S(2)}, u32[]{:S(2)}) async-start(bf16[128,2,1,256]{3,1,2,0:T(2,128)(2,1)} %copy.119), calls=%async_computation.4 | async-start | bytes 262144 | tf_op jit(solution)/shard_map/all_to_all | solution.py:88
  282.3 1.2 fusion.43
  283.6 10.4 %all-to-all-done.4 = bf16[128,2,1,256]{3,1,2,0:T(2,128)(2,1)S(1)} async-done(((bf16[128,2,1,256]{3,1,2,0:T(2,128)(2,1)}), bf16[128,2,1,256]{3,1,2,0:T(2,128)(2,1)S(1)}, u32[]{:S(2)}, u32[]{:S(2)}) %all-to-all-start.4) | async-done | bytes 131104 | tf_op jit(solution)/shard_map/all_to_all | solution.py:88
  294.0 0.9 broadcast_in_dim.33
  295.0 9.0 %all-to-all-start.10 = ((bf16[4,2,196,128]{3,1,2,0:T(2,128)(2,1)}), bf16[4,2,196,128]{3,1,2,0:T(2,128)(2,1)S(1)}, u32[]{:S(2)}, u32[]{:S(2)}) async-start(bf16[4,2,196,128]{3,1,2,0:T(2,128)(2,1)} %broadcast_in_dim.33), calls=%async_computation.10 | async-start | bytes 802816 | tf_op jit(solution)/shard_map/all_to_all | solution.py:11
  304.3 28.1 %all-to-all-done.10 = bf16[4,2,196,128]{3,1,2,0:T(2,128)(2,1)S(1)} async-done(((bf16[4,2,196,128]{3,1,2,0:T(2,128)(2,1)}), bf16[4,2,196,128]{3,1,2,0:T(2,128)(2,1)S(1)}, u32[]{:S(2)}, u32[]{:S(2)}) %all-to-all-start.10) | async-done | bytes 401440 | tf_op jit(solution)/shard_map/all_to_all | solution.py:11
  332.4 0.9 broadcast_in_dim.14
  333.4 4.0 %all-to-all-start.5 = ((bf16[4,2,196,128]{3,1,2,0:T(2,128)(2,1)}), bf16[4,2,196,128]{3,1,2,0:T(2,128)(2,1)S(1)}, u32[]{:S(2)}, u32[]{:S(2)}) async-start(bf16[4,2,196,128]{3,1,2,0:T(2,128)(2,1)} %broadcast_in_dim.14), calls=%async_computation.5 | async-start | bytes 802816 | tf_op jit(solution)/shard_map/all_to_all | solution.py:11
  338.9 0.8 copy.136
  340.2 1.2 multiply_reduce_fusion
  341.3 16.2 %all-to-all-done.5 = bf16[4,2,196,128]{3,1,2,0:T(2,128)(2,1)S(1)} async-done(((bf16[4,2,196,128]{3,1,2,0:T(2,128)(2,1)}), bf16[4,2,196,128]{3,1,2,0:T(2,128)(2,1)S(1)}, u32[]{:S(2)}, u32[]{:S(2)}) %all-to-all-start.5) | async-done | bytes 401440 | tf_op jit(solution)/shard_map/all_to_all | solution.py:11
  357.9 3.9 %fusion.41 = bf16[2,196,128]{2,0,1:T(2,128)(2,1)S(1)} fusion(f32[2,196,128]{2,0,1:T(2,128)} %get-tuple-element.27, f32[2,196,128]{2,0,1:T(2,128)S(1)} %convert_reduce_fusion.2, f32[2,196,128]{2,0,1:T(2,128)} %get-tuple-element.33, f32[2,196,128]{2,0,1:T(2,128)S(1)} %convert_reduce_fusion.1, f32[2,128]{1,0:T(2,128)S(1)} %multiply_reduce_fusion, ...), kind=kOutput, calls=%fused_computation.31 | output fusion | flops 401927 | bytes 905760 | tf_op jit(solution)/shard_map/sub | solution.py:129
  362.0 1.1 fusion.36
  363.1 0.8 copy.137
  (31 shorter events, 4.7 us)
Async XLA Ops:
  0.6 159.8 %copy-start = (bf16[1,1024,1024]{2,1,0:T(8,128)(2,1)S(1)}, bf16[1,1024,1024]{2,1,0:T(8,128)(2,1)}, u32[]{:S(2)}) copy-start(bf16[1,1024,1024]{2,1,0:T(8,128)(2,1)} %param.9) | copy-start | bytes 6291460
  63.2 15.9 %copy-start.2 = (bf16[2,196,256]{2,0,1:T(2,128)(2,1)S(1)}, bf16[2,196,256]{2,0,1:T(2,128)(2,1)}, u32[]{:S(2)}) copy-start(bf16[2,196,256]{2,0,1:T(2,128)(2,1)} %param.13) | copy-start | bytes 602116
  67.6 23.2 %all-to-all-start.1 = ((bf16[2,128,256]{2,0,1:T(2,128)(2,1)}), bf16[2,128,256]{2,0,1:T(2,128)(2,1)S(1)}, u32[]{:S(2)}, u32[]{:S(2)}) async-start(bf16[2,128,256]{2,0,1:T(2,128)(2,1)} %copy.114), calls=%async_computation.1 | async-start | bytes 262144 | tf_op jit(solution)/shard_map/all_to_all | solution.py:75
  90.8 23.3 %all-to-all-start.6 = ((bf16[2,128,256]{2,0,1:T(2,128)(2,1)}), bf16[2,128,256]{2,0,1:T(2,128)(2,1)S(1)}, u32[]{:S(2)}, u32[]{:S(2)}) async-start(bf16[2,128,256]{2,0,1:T(2,128)(2,1)} %copy.126), calls=%async_computation.6 | async-start | bytes 262144 | tf_op jit(solution)/shard_map/all_to_all | solution.py:105
  114.9 39.9 %all-to-all-start.2 = ((bf16[4,256,1,256]{1,3,2,0:T(8,128)(2,1)}), bf16[4,256,1,256]{1,3,2,0:T(8,128)(2,1)S(1)}, u32[]{:S(2)}, u32[]{:S(2)}) async-start(bf16[4,256,1,256]{1,3,2,0:T(8,128)(2,1)} %broadcast_in_dim.13), calls=%async_computation.2 | async-start | bytes 1048576 | tf_op jit(solution)/shard_map/all_to_all | solution.py:11
  155.7 25.6 %all-to-all-start.7 = ((bf16[4,256,1,256]{1,3,2,0:T(8,128)(2,1)}), bf16[4,256,1,256]{1,3,2,0:T(8,128)(2,1)S(1)}, u32[]{:S(2)}, u32[]{:S(2)}) async-start(bf16[4,256,1,256]{1,3,2,0:T(8,128)(2,1)} %broadcast_in_dim.32), calls=%async_computation.7 | async-start | bytes 1048576 | tf_op jit(solution)/shard_map/all_to_all | solution.py:11
  185.8 29.8 %all-to-all-start.8 = ((bf16[4,256,1,256]{3,1,2,0:T(8,128)(2,1)}), bf16[4,256,1,256]{3,1,2,0:T(8,128)(2,1)S(1)}, u32[]{:S(2)}, u32[]{:S(2)}) async-start(bf16[4,256,1,256]{3,1,2,0:T(8,128)(2,1)} %bitcast.134), calls=%async_computation.8 | async-start | bytes 1048576 | tf_op jit(solution)/shard_map/all_to_all | solution.py:37
  215.6 25.2 %all-to-all-start.3 = ((bf16[4,256,1,256]{3,1,2,0:T(8,128)(2,1)}), bf16[4,256,1,256]{3,1,2,0:T(8,128)(2,1)S(1)}, u32[]{:S(2)}, u32[]{:S(2)}) async-start(bf16[4,256,1,256]{3,1,2,0:T(8,128)(2,1)} %bitcast.138), calls=%async_computation.3 | async-start | bytes 1048576 | tf_op jit(solution)/shard_map/all_to_all | solution.py:37
  240.8 31.3 %all-to-all-start.9 = ((bf16[128,2,1,256]{3,1,2,0:T(2,128)(2,1)}), bf16[128,2,1,256]{3,1,2,0:T(2,128)(2,1)}, u32[]{:S(2)}, u32[]{:S(2)}) async-start(bf16[128,2,1,256]{3,1,2,0:T(2,128)(2,1)} %bitcast.37), calls=%async_computation.9 | async-start | bytes 262144 | tf_op jit(solution)/shard_map/all_to_all | solution.py:115
  260.7 43.2 %copy-start.3 = (bf16[2,196,256]{2,0,1:T(2,128)(2,1)S(1)}, bf16[2,196,256]{2,0,1:T(2,128)(2,1)}, u32[]{:S(2)}) copy-start(bf16[2,196,256]{2,0,1:T(2,128)(2,1)} %param.13) | copy-start | bytes 602116
  272.1 22.0 %all-to-all-start.4 = ((bf16[128,2,1,256]{3,1,2,0:T(2,128)(2,1)}), bf16[128,2,1,256]{3,1,2,0:T(2,128)(2,1)S(1)}, u32[]{:S(2)}, u32[]{:S(2)}) async-start(bf16[128,2,1,256]{3,1,2,0:T(2,128)(2,1)} %copy.119), calls=%async_computation.4 | async-start | bytes 262144 | tf_op jit(solution)/shard_map/all_to_all | solution.py:88
  295.0 37.4 %all-to-all-start.10 = ((bf16[4,2,196,128]{3,1,2,0:T(2,128)(2,1)}), bf16[4,2,196,128]{3,1,2,0:T(2,128)(2,1)S(1)}, u32[]{:S(2)}, u32[]{:S(2)}) async-start(bf16[4,2,196,128]{3,1,2,0:T(2,128)(2,1)} %broadcast_in_dim.33), calls=%async_computation.10 | async-start | bytes 802816 | tf_op jit(solution)/shard_map/all_to_all | solution.py:11
  333.4 24.1 %all-to-all-start.5 = ((bf16[4,2,196,128]{3,1,2,0:T(2,128)(2,1)}), bf16[4,2,196,128]{3,1,2,0:T(2,128)(2,1)S(1)}, u32[]{:S(2)}, u32[]{:S(2)}) async-start(bf16[4,2,196,128]{3,1,2,0:T(2,128)(2,1)} %broadcast_in_dim.14), calls=%async_computation.5 | async-start | bytes 802816 | tf_op jit(solution)/shard_map/all_to_all | solution.py:11
  338.1 19.8 %copy-start.4 = (f32[2,196]{0,1:T(8,128)S(1)}, f32[2,196]{0,1:T(8,128)}, u32[]{:S(2)}) copy-start(f32[2,196]{0,1:T(8,128)} %get-tuple-element.31) | copy-start | bytes 4708
  339.8 22.0 %copy-start.1 = (bf16[256,128]{1,0:T(8,128)(2,1)S(1)}, bf16[256,128]{1,0:T(8,128)(2,1)}, u32[]{:S(2)}) copy-start(bf16[256,128]{1,0:T(8,128)(2,1)} %param.8) | copy-start | bytes 196612
where the time goes:
time: 365 us; the launch traced here: 364 us
  waiting for transfers between devices  176 us (48%)
  starting transfers between devices  87.7 us (24%)
  blocking collectives  60.5 us (17%)
  matrix products  13.7 us (4%)
  other arithmetic  12.8 us (4%)
  local copies, waits for them, and re-layouts  12.5 us (3%)
    all_to_all x4, waiting for transfers between devices, sent_to_all(): return lax.all_to_all(copies, axis, split_axis=0, concat_axis=0, tiled=True)  96.9 us
    all_to_all x1, blocking collectives, sent_to_all(): return lax.all_to_all(copies, axis, split_axis=0, concat_axis=0, tiled=True)  60.5 us
    all_to_all x2, waiting for transfers between devices, sent_and_summed(): tiles = lax.all_to_all(split_up(x, dim, peers), axis, 0, 0, tiled=True)  36.8 us
    all_to_all x4, starting transfers between devices, sent_to_all(): return lax.all_to_all(copies, axis, split_axis=0, concat_axis=0, tiled=True)  23.4 us
    all_to_all x1, starting transfers between devices, per_device(): lax.all_to_all(slot_grad.reshape(groups, images_dev, local_experts, quart...  18.6 us
    all_to_all x2, starting transfers between devices, sent_and_summed(): tiles = lax.all_to_all(split_up(x, dim, peers), axis, 0, 0, tiled=True)  12.3 us
    all_to_all x1, starting transfers between devices, per_device(): lax.all_to_all(out_grad, 'expert', split_axis=1, concat_axis=0, tiled=True)  11.6 us
    all_to_all x1, starting transfers between devices, per_device(): lax.all_to_all(slot_in, 'expert', split_axis=1, concat_axis=0, tiled=True)  11.5 us
  transfers between devices with their start and end apart: 10, of which 10 were waited for; matrix products, arithmetic and copies ran while one was open for 5% of the time, Pallas kernels for 0%

commit v1 on v0

--- a/solution.py
+++ b/solution.py
@@ -102,7 +102,9 @@
     out_grad = jnp.einsum(
         "its,itd->isd", combine_low, cotangent, preferred_element_type=jnp.float32
     ).astype(jnp.bfloat16)
-    grad_arrived = lax.all_to_all(out_grad, "expert", split_axis=1, concat_axis=0, tiled=True)
+    pieces = jnp.split(out_grad, lax.axis_size("expert"), axis=1)
+    received = lax.all_to_all(jnp.stack(pieces), "expert", 0, 0)
+    grad_arrived = jnp.concatenate(received, axis=0)
     hidden_grad = jnp.einsum(
         "ren,efn->ref",
         gathered_copies(grad_arrived, "hidden", 2),

time: 365 us -> 433 us (1.19)
  local copies, waits for them, and re-layouts: 12.5 us -> 89.5 us
  waiting for transfers between devices: 176 us -> 160 us
  starting transfers between devices: 87.7 us -> 95.3 us
    unnamed x13 -> x144, local copies, waits for them, and re-layouts: 2.36 us -> 76.2 us
    all_to_all x1, waiting for transfers between devices: 10.7 us -> 0.01 us  [per_device(): lax.all_to_all(slot_in, 'expert', split_axis=1, concat_axis=0, tiled=True)]
    all_to_all x2, waiting for transfers between devices: 36.8 us -> 29.9 us  [sent_and_summed(): tiles = lax.all_to_all(split_up(x, dim, peers), axis, 0, 0, tiled=True)]
    all_to_all x1, starting transfers between devices: 18.6 us -> 23.2 us  [per_device(): lax.all_to_all(slot_grad.reshape(groups, images_dev, local_experts, quart...]
    all_to_all x1, starting transfers between devices: 11.6 us -> 16 us  [per_device(): received = lax.all_to_all(jnp.stack(pieces), 'expert', 0, 0)]
  transfers between devices with their start and end apart: 10 -> 10, of which waited for: 10 -> 9; matrix products, arithmetic and copies ran while one was open for 5% -> 21% of each run, Pallas kernels for 0% -> 0%
where the time goes in v1:
time: 433 us; the launch traced here: 432 us
  waiting for transfers between devices  160 us (37%)
  starting transfers between devices  95.3 us (22%)
  local copies, waits for them, and re-layouts  89.5 us (21%)
  blocking collectives  60.5 us (14%)
  matrix products  15.3 us (4%)
  other arithmetic  10.5 us (2%)
    all_to_all x4, waiting for transfers between devices, sent_to_all(): return lax.all_to_all(copies, axis, split_axis=0, concat_axis=0, tiled=True)  96.8 us
    unnamed x144, local copies, waits for them, and re-layouts  76.2 us
    all_to_all x1, blocking collectives, sent_to_all(): return lax.all_to_all(copies, axis, split_axis=0, concat_axis=0, tiled=True)  60.5 us
    all_to_all x2, waiting for transfers between devices, sent_and_summed(): tiles = lax.all_to_all(split_up(x, dim, peers), axis, 0, 0, tiled=True)  29.9 us
    all_to_all x1, starting transfers between devices, per_device(): lax.all_to_all(slot_grad.reshape(groups, images_dev, local_experts, quart...  23.2 us
    all_to_all x4, starting transfers between devices, sent_to_all(): return lax.all_to_all(copies, axis, split_axis=0, concat_axis=0, tiled=True)  22 us
    all_to_all x1, starting transfers between devices, per_device(): received = lax.all_to_all(jnp.stack(pieces), 'expert', 0, 0)  16 us
    all_to_all x2, starting transfers between devices, sent_and_summed(): tiles = lax.all_to_all(split_up(x, dim, peers), axis, 0, 0, tiled=True)  12.2 us
  transfers between devices with their start and end apart: 10, of which 9 were waited for; matrix products, arithmetic and copies ran while one was open for 21% of the time, Pallas kernels for 0%

profile of v1, /device:TPU:49, one launch (start us, length us, event | category | flops | bytes accessed | tf_op | source)
XLA Modules:
  0.0 432.1 jit_solution(6445667042676074697)
XLA Ops:
  0.6 1.3 fusion.72
  2.3 60.5 %all_to_all.88 = f32[4,2,196,128]{3,1,2,0:T(2,128)S(1)} all-to-all(f32[4,2,196,128]{3,1,2,0:T(2,128)S(1)} %broadcast_in_dim.12), channel_id=1, replica_groups=mesh['expert'=128,'hidden'=4] {'hidden'}, dimensions={0} | all-to-all | bytes 1605632 | tf_op jit(solution)/shard_map/all_to_all | solution.py:11
  63.5 1.4 exponential_reduce_fusion
  64.9 1.2 fusion.105
  66.0 1.2 convolution_convert_fusion.1
  68.3 0.8 copy.3948
  69.1 11.5 %all-to-all-start.1 = ((bf16[2,128,256]{2,0,1:T(2,128)(2,1)}), bf16[2,128,256]{2,0,1:T(2,128)(2,1)S(1)}, u32[]{:S(2)}, u32[]{:S(2)}) async-start(bf16[2,128,256]{2,0,1:T(2,128)(2,1)} %copy.3948), calls=%async_computation.1 | async-start | bytes 262144 | tf_op jit(solution)/shard_map/all_to_all | solution.py:75
  102.5 0.6 constant_dynamic-update-slice_fusion.88
  135.9 0.6 constant_dynamic-update-slice_fusion.30
  153.7 16.0 %all-to-all-start.6 = ((bf16[128,2,1,256]{3,1,2,0:T(2,128)(2,1)}), bf16[128,2,1,256]{3,1,2,0:T(2,128)(2,1)S(1)}, u32[]{:S(2)}, u32[]{:S(2)}) async-start(bf16[128,2,1,256]{3,1,2,0:T(2,128)(2,1)} %constant_dynamic-update-slice_fusion), calls=%async_computation.6 | async-start | bytes 262144 | tf_op jit(solution)/shard_map/all_to_all | solution.py:106
  170.0 11.3 %all-to-all-done.6 = bf16[128,2,1,256]{3,1,2,0:T(2,128)(2,1)S(1)} async-done(((bf16[128,2,1,256]{3,1,2,0:T(2,128)(2,1)}), bf16[128,2,1,256]{3,1,2,0:T(2,128)(2,1)S(1)}, u32[]{:S(2)}, u32[]{:S(2)}) %all-to-all-start.6) | async-done | bytes 131104 | tf_op jit(solution)/shard_map/all_to_all | solution.py:106
  181.3 0.8 broadcast_in_dim.13
  182.1 6.4 %all-to-all-start.2 = ((bf16[4,256,1,256]{1,3,2,0:T(8,128)(2,1)}), bf16[4,256,1,256]{1,3,2,0:T(8,128)(2,1)S(1)}, u32[]{:S(2)}, u32[]{:S(2)}) async-start(bf16[4,256,1,256]{1,3,2,0:T(8,128)(2,1)} %broadcast_in_dim.13), calls=%async_computation.2 | async-start | bytes 1048576 | tf_op jit(solution)/shard_map/all_to_all | solution.py:11
  188.7 33.4 %all-to-all-done.2 = bf16[4,256,1,256]{1,3,2,0:T(8,128)(2,1)S(1)} async-done(((bf16[4,256,1,256]{1,3,2,0:T(8,128)(2,1)}), bf16[4,256,1,256]{1,3,2,0:T(8,128)(2,1)S(1)}, u32[]{:S(2)}, u32[]{:S(2)}) %all-to-all-start.2) | async-done | bytes 524320 | tf_op jit(solution)/shard_map/all_to_all | solution.py:11
  222.1 0.8 broadcast_in_dim.32
  223.0 4.0 all-to-all-start.7
  227.0 1.7 fusion.21
  228.7 19.8 %all-to-all-done.7 = bf16[4,256,1,256]{1,3,2,0:T(8,128)(2,1)S(1)} async-done(((bf16[4,256,1,256]{1,3,2,0:T(8,128)(2,1)}), bf16[4,256,1,256]{1,3,2,0:T(8,128)(2,1)S(1)}, u32[]{:S(2)}, u32[]{:S(2)}) %all-to-all-start.7) | async-done | bytes 524320 | tf_op jit(solution)/shard_map/all_to_all | solution.py:11
  248.6 4.5 %fusion.39 = bf16[256,1,1024]{2,0,1:T(8,128)(2,1)} fusion(bf16[1,1024,1024]{2,1,0:T(8,128)(2,1)S(1)} %copy-done, bf16[256,1024]{0,1:T(8,128)(2,1)S(1)} %bitcast.393, bf16[1,1024,1024]{2,1,0:T(8,128)(2,1)} %param.11, f32[256,1,1024]{2,0,1:T(8,128)} %fusion.21), kind=kOutput, calls=%fused_computation.21 | convolution fusion | flops 1078984704 | bytes 6291456 | tf_op jit(solution)/shard_map/ref,ekf->rek/dot_general | solution.py:115
  253.1 1.4 reshape.124
  254.5 0.9 copy.3964
  255.4 8.2 %all-to-all-start.8 = ((bf16[4,256,1,256]{3,1,2,0:T(8,128)(2,1)}), bf16[4,256,1,256]{3,1,2,0:T(8,128)(2,1)S(1)}, u32[]{:S(2)}, u32[]{:S(2)}) async-start(bf16[4,256,1,256]{3,1,2,0:T(8,128)(2,1)} %copy.3964), calls=%async_computation.8 | async-start | bytes 1048576 | tf_op jit(solution)/shard_map/all_to_all | solution.py:37
  263.5 3.5 fusion.36
  267.1 1.4 reshape.119
  268.5 0.9 copy.3953
  269.4 15.7 %all-to-all-done.8 = bf16[4,256,1,256]{3,1,2,0:T(8,128)(2,1)S(1)} async-done(((bf16[4,256,1,256]{3,1,2,0:T(8,128)(2,1)}), bf16[4,256,1,256]{3,1,2,0:T(8,128)(2,1)S(1)}, u32[]{:S(2)}, u32[]{:S(2)}) %all-to-all-start.8) | async-done | bytes 524320 | tf_op jit(solution)/shard_map/all_to_all | solution.py:37
  285.1 4.1 all-to-all-start.3
  289.2 0.7 reduce_sum.103
  289.9 1.6 reshape.125
  291.5 14.2 %all-to-all-done.3 = bf16[4,256,1,256]{3,1,2,0:T(8,128)(2,1)S(1)} async-done(((bf16[4,256,1,256]{3,1,2,0:T(8,128)(2,1)}), bf16[4,256,1,256]{3,1,2,0:T(8,128)(2,1)S(1)}, u32[]{:S(2)}, u32[]{:S(2)}) %all-to-all-start.3) | async-done | bytes 524320 | tf_op jit(solution)/shard_map/all_to_all | solution.py:37
  305.7 23.2 %all-to-all-start.9 = ((bf16[128,2,1,256]{3,1,2,0:T(2,128)(2,1)}), bf16[128,2,1,256]{3,1,2,0:T(2,128)(2,1)}, u32[]{:S(2)}, u32[]{:S(2)}) async-start(bf16[128,2,1,256]{3,1,2,0:T(2,128)(2,1)} %bitcast.35), calls=%async_computation.9 | async-start | bytes 262144 | tf_op jit(solution)/shard_map/all_to_all | solution.py:117
  329.2 0.8 copy.3955
  330.0 11.5 %all-to-all-done.9 = bf16[128,2,1,256]{3,1,2,0:T(2,128)(2,1)} async-done(((bf16[128,2,1,256]{3,1,2,0:T(2,128)(2,1)}), bf16[128,2,1,256]{3,1,2,0:T(2,128)(2,1)}, u32[]{:S(2)}, u32[]{:S(2)}) %all-to-all-start.9) | async-done | bytes 131104 | tf_op jit(solution)/shard_map/all_to_all | solution.py:117
  341.5 10.3 %all-to-all-start.4 = ((bf16[128,2,1,256]{3,1,2,0:T(2,128)(2,1)}), bf16[128,2,1,256]{3,1,2,0:T(2,128)(2,1)S(1)}, u32[]{:S(2)}, u32[]{:S(2)}) async-start(bf16[128,2,1,256]{3,1,2,0:T(2,128)(2,1)} %copy.3955), calls=%async_computation.4 | async-start | bytes 262144 | tf_op jit(solution)/shard_map/all_to_all | solution.py:88
  351.8 1.2 fusion.49
  353.1 10.4 %all-to-all-done.4 = bf16[128,2,1,256]{3,1,2,0:T(2,128)(2,1)S(1)} async-done(((bf16[128,2,1,256]{3,1,2,0:T(2,128)(2,1)}), bf16[128,2,1,256]{3,1,2,0:T(2,128)(2,1)S(1)}, u32[]{:S(2)}, u32[]{:S(2)}) %all-to-all-start.4) | async-done | bytes 131104 | tf_op jit(solution)/shard_map/all_to_all | solution.py:88
  363.5 1.0 broadcast_in_dim.33
  364.5 7.6 %all-to-all-start.10 = ((bf16[4,2,196,128]{3,1,2,0:T(2,128)(2,1)}), bf16[4,2,196,128]{3,1,2,0:T(2,128)(2,1)S(1)}, u32[]{:S(2)}, u32[]{:S(2)}) async-start(bf16[4,2,196,128]{3,1,2,0:T(2,128)(2,1)} %broadcast_in_dim.33), calls=%async_computation.10 | async-start | bytes 802816 | tf_op jit(solution)/shard_map/all_to_all | solution.py:11
  372.4 28.2 %all-to-all-done.10 = bf16[4,2,196,128]{3,1,2,0:T(2,128)(2,1)S(1)} async-done(((bf16[4,2,196,128]{3,1,2,0:T(2,128)(2,1)}), bf16[4,2,196,128]{3,1,2,0:T(2,128)(2,1)S(1)}, u32[]{:S(2)}, u32[]{:S(2)}) %all-to-all-start.10) | async-done | bytes 401440 | tf_op jit(solution)/shard_map/all_to_all | solution.py:11
  400.5 1.0 broadcast_in_dim.14
  401.5 4.0 all-to-all-start.5
  405.5 1.6 multiply_multiply_fusion.1
  407.1 1.6 copy.3973
  408.9 0.8 copy.3971
  410.3 15.4 %all-to-all-done.5 = bf16[4,2,196,128]{3,1,2,0:T(2,128)(2,1)S(1)} async-done(((bf16[4,2,196,128]{3,1,2,0:T(2,128)(2,1)}), bf16[4,2,196,128]{3,1,2,0:T(2,128)(2,1)S(1)}, u32[]{:S(2)}, u32[]{:S(2)}) %all-to-all-start.5) | async-done | bytes 401440 | tf_op jit(solution)/shard_map/all_to_all | solution.py:11
  426.1 3.8 fusion.47
  430.2 1.1 fusion.42
  431.3 0.8 copy.3972
  (173 shorter events, 76.4 us)
Async XLA Ops:
  0.6 226.4 %copy-start = (bf16[1,1024,1024]{2,1,0:T(8,128)(2,1)S(1)}, bf16[1,1024,1024]{2,1,0:T(8,128)(2,1)}, u32[]{:S(2)}) copy-start(bf16[1,1024,1024]{2,1,0:T(8,128)(2,1)} %param.9) | copy-start | bytes 6291460
  63.2 4.9 %copy-start.1 = (bf16[2,196,256]{2,0,1:T(2,128)(2,1)S(1)}, bf16[2,196,256]{2,0,1:T(2,128)(2,1)}, u32[]{:S(2)}) copy-start(bf16[2,196,256]{2,0,1:T(2,128)(2,1)} %param.7) | copy-start | bytes 602116
  69.1 84.5 %all-to-all-start.1 = ((bf16[2,128,256]{2,0,1:T(2,128)(2,1)}), bf16[2,128,256]{2,0,1:T(2,128)(2,1)S(1)}, u32[]{:S(2)}, u32[]{:S(2)}) async-start(bf16[2,128,256]{2,0,1:T(2,128)(2,1)} %copy.3948), calls=%async_computation.1 | async-start | bytes 262144 | tf_op jit(solution)/shard_map/all_to_all | solution.py:75
  153.7 27.6 %all-to-all-start.6 = ((bf16[128,2,1,256]{3,1,2,0:T(2,128)(2,1)}), bf16[128,2,1,256]{3,1,2,0:T(2,128)(2,1)S(1)}, u32[]{:S(2)}, u32[]{:S(2)}) async-start(bf16[128,2,1,256]{3,1,2,0:T(2,128)(2,1)} %constant_dynamic-update-slice_fusion), calls=%async_computation.6 | async-start | bytes 262144 | tf_op jit(solution)/shard_map/all_to_all | solution.py:106
  169.9 57.1 %copy-start.5 = (bf16[1,1024]{1,0:T(2,128)(2,1)S(1)}, bf16[1,1024]{1,0:T(2,128)(2,1)}, u32[]{:S(2)}) copy-start(bf16[1,1024]{1,0:T(2,128)(2,1)} %param.10) | copy-start | bytes 6148
  182.1 40.0 %all-to-all-start.2 = ((bf16[4,256,1,256]{1,3,2,0:T(8,128)(2,1)}), bf16[4,256,1,256]{1,3,2,0:T(8,128)(2,1)S(1)}, u32[]{:S(2)}, u32[]{:S(2)}) async-start(bf16[4,256,1,256]{1,3,2,0:T(8,128)(2,1)} %broadcast_in_dim.13), calls=%async_computation.2 | async-start | bytes 1048576 | tf_op jit(solution)/shard_map/all_to_all | solution.py:11
  223.0 25.6 %all-to-all-start.7 = ((bf16[4,256,1,256]{1,3,2,0:T(8,128)(2,1)}), bf16[4,256,1,256]{1,3,2,0:T(8,128)(2,1)S(1)}, u32[]{:S(2)}, u32[]{:S(2)}) async-start(bf16[4,256,1,256]{1,3,2,0:T(8,128)(2,1)} %broadcast_in_dim.32), calls=%async_computation.7 | async-start | bytes 1048576 | tf_op jit(solution)/shard_map/all_to_all | solution.py:11
  255.4 29.7 %all-to-all-start.8 = ((bf16[4,256,1,256]{3,1,2,0:T(8,128)(2,1)}), bf16[4,256,1,256]{3,1,2,0:T(8,128)(2,1)S(1)}, u32[]{:S(2)}, u32[]{:S(2)}) async-start(bf16[4,256,1,256]{3,1,2,0:T(8,128)(2,1)} %copy.3964), calls=%async_computation.8 | async-start | bytes 1048576 | tf_op jit(solution)/shard_map/all_to_all | solution.py:37
  267.1 61.9 %copy-start.6 = (bf16[1,256]{1,0:T(2,128)(2,1)S(1)}, bf16[1,256]{1,0:T(2,128)(2,1)}, u32[]{:S(2)}) copy-start(bf16[1,256]{1,0:T(2,128)(2,1)} %param.12) | copy-start | bytes 1540
  285.1 20.6 %all-to-all-start.3 = ((bf16[4,256,1,256]{3,1,2,0:T(8,128)(2,1)}), bf16[4,256,1,256]{3,1,2,0:T(8,128)(2,1)S(1)}, u32[]{:S(2)}, u32[]{:S(2)}) async-start(bf16[4,256,1,256]{3,1,2,0:T(8,128)(2,1)} %copy.3953), calls=%async_computation.3 | async-start | bytes 1048576 | tf_op jit(solution)/shard_map/all_to_all | solution.py:37
  305.7 35.8 %all-to-all-start.9 = ((bf16[128,2,1,256]{3,1,2,0:T(2,128)(2,1)}), bf16[128,2,1,256]{3,1,2,0:T(2,128)(2,1)}, u32[]{:S(2)}, u32[]{:S(2)}) async-start(bf16[128,2,1,256]{3,1,2,0:T(2,128)(2,1)} %bitcast.35), calls=%async_computation.9 | async-start | bytes 262144 | tf_op jit(solution)/shard_map/all_to_all | solution.py:117
  329.0 43.0 %copy-start.4 = (bf16[2,196,256]{2,0,1:T(2,128)(2,1)S(1)}, bf16[2,196,256]{2,0,1:T(2,128)(2,1)}, u32[]{:S(2)}) copy-start(bf16[2,196,256]{2,0,1:T(2,128)(2,1)} %param.13) | copy-start | bytes 602116
  341.5 22.0 %all-to-all-start.4 = ((bf16[128,2,1,256]{3,1,2,0:T(2,128)(2,1)}), bf16[128,2,1,256]{3,1,2,0:T(2,128)(2,1)S(1)}, u32[]{:S(2)}, u32[]{:S(2)}) async-start(bf16[128,2,1,256]{3,1,2,0:T(2,128)(2,1)} %copy.3955), calls=%async_computation.4 | async-start | bytes 262144 | tf_op jit(solution)/shard_map/all_to_all | solution.py:88
  364.5 36.0 %all-to-all-start.10 = ((bf16[4,2,196,128]{3,1,2,0:T(2,128)(2,1)}), bf16[4,2,196,128]{3,1,2,0:T(2,128)(2,1)S(1)}, u32[]{:S(2)}, u32[]{:S(2)}) async-start(bf16[4,2,196,128]{3,1,2,0:T(2,128)(2,1)} %broadcast_in_dim.33), calls=%async_computation.10 | async-start | bytes 802816 | tf_op jit(solution)/shard_map/all_to_all | solution.py:11
  372.1 38.0 %copy-start.2 = (f32[2,196,128]{2,0,1:T(2,128)S(1)}, f32[2,196,128]{2,0,1:T(2,128)}, u32[]{:S(2)}) copy-start(f32[2,196,128]{2,0,1:T(2,128)} %get-tuple-element.123) | copy-start | bytes 602116
  401.5 24.2 %all-to-all-start.5 = ((bf16[4,2,196,128]{3,1,2,0:T(2,128)(2,1)}), bf16[4,2,196,128]{3,1,2,0:T(2,128)(2,1)S(1)}, u32[]{:S(2)}, u32[]{:S(2)}) async-start(bf16[4,2,196,128]{3,1,2,0:T(2,128)(2,1)} %broadcast_in_dim.14), calls=%async_computation.5 | async-start | bytes 802816 | tf_op jit(solution)/shard_map/all_to_all | solution.py:11
  409.7 20.2 %copy-start.3 = (bf16[256,128]{1,0:T(8,128)(2,1)S(1)}, bf16[256,128]{1,0:T(8,128)(2,1)}, u32[]{:S(2)}) copy-start(bf16[256,128]{1,0:T(8,128)(2,1)} %param.8) | copy-start | bytes 196612
